TPU v7x, 32 devices: a whole 2x2x4 slice. The times are simulated.
32 devices in a mesh: row: 4 (over y, core), col: 8 (over z, x).
Axes of the slice: x: 2, y: 2, z: 4, core: 2. Of those that a mesh axis runs over, the one named last changes fastest.
Arguments:
- inverse: float32 [16384, 16384], P('row', 'col'), may hold values from -6 to 6
- front_blocks: int32 [2, 16], replicated, may hold values from 0 to 63, as said below
- panels: float32 [2, 4096, 256], P(None, 'row'), may hold values from -0.09375 to 0.09375
- diag_terms: float32 [2, 256, 256], replicated, may hold values from -6 to 6
- bounds: int32 [2, 4], replicated, may hold values from 1 to 128, 256 in all within a row
Outputs:
- border: float32 [2, 4096, 256], P(None, ('row', 'col'))
- diag_block: float32 [2, 256, 256], replicated
Inputs may be any that keep to these rules, and one draw needn't show every extreme that they name: `front_blocks`: each row names 16 distinct blocks. Positions 4 r to 4 r + 3 name blocks of four different groups of 16 consecutive blocks, and every such group is named at exactly four positions, of four different r. Positions 2 o and 2 o + 1 name blocks of two different groups of 8 consecutive blocks, and every such group is named at exactly two positions, of two different o.
All inputs are finite; a program needn't handle non-finite values.
Results may differ from a plain program's by a relative error of at most 0.0001.
Values sent between devices are 32-bit elements; how exact they have to be, the bound alone decides.
A program may use at most 128 MiB of HBM per device.

v0:
```python
import jax
import jax.numpy as jnp
from jax import lax
from jax.sharding import PartitionSpec as P

BS = 256


def body(inverse, front_blocks, panels, diag_terms, bounds):
    n_row = lax.axis_size("row")
    n_col = lax.axis_size("col")
    row_index = lax.axis_index("row")
    col_index = lax.axis_index("col")
    rows_loc, cols_loc = inverse.shape
    row_group = rows_loc // BS
    col_group = cols_loc // BS
    list_length = front_blocks.shape[1]
    per_owner = list_length // n_row
    highest = lax.Precision.HIGHEST
    borders = []
    diagonals = []
    for front_index in range(2):
        front_list = front_blocks[front_index]
        own_blocks = lax.dynamic_slice_in_dim(front_list, row_index * per_owner, per_owner)
        w_loc = panels[front_index]
        panel_width = w_loc.shape[1]
        w_pieces = w_loc.reshape(per_owner, BS, panel_width)
        targets = col_index * col_group + jnp.arange(col_group, dtype=jnp.int32)
        picker = (own_blocks[None, :] == targets[:, None]).astype(jnp.float32)
        own_piece = jnp.einsum("ki,iab->ab", picker, w_pieces, precision=highest)
        slot_rows = lax.all_gather(own_piece, "row", axis=0, tiled=True).reshape(
            n_row, BS, panel_width
        )
        owners = front_list.reshape(n_row, per_owner)
        placer = jnp.sum((owners[None, :, :] == targets[:, None, None]).astype(jnp.float32), axis=2)
        w_tilde = jnp.einsum("ks,sab->kab", placer, slot_rows, precision=highest).reshape(
            cols_loc, panel_width
        )
        dest_lists = front_list.reshape(n_row, per_owner)
        local_ids = row_index * row_group + jnp.arange(row_group, dtype=jnp.int32)
        share_rows = per_owner * BS // n_col
        full_rows = jnp.dot(inverse, w_tilde, precision=highest)
        quarters = BS // share_rows
        full_pieces = full_rows.reshape(row_group, quarters, share_rows, panel_width)
        first_rows = jnp.arange(n_col, dtype=jnp.int32) * share_rows
        dest_block = dest_lists[:, first_rows // BS]
        block_pick = (dest_block.T[:, :, None] == local_ids[None, None, :]).astype(jnp.float32)
        quarter_pick = (
            (first_rows % BS // share_rows)[:, None]
            == jnp.arange(quarters, dtype=jnp.int32)[None, :]
        ).astype(jnp.float32)
        sectioned = jnp.einsum("cq,kqap->ckap", quarter_pick, full_pieces, precision=highest)
        ordered = jnp.einsum("cdk,ckap->cdap", block_pick, sectioned, precision=highest)
        ordered = ordered.reshape(n_col * n_row * share_rows, panel_width)
        reduced = lax.psum_scatter(ordered, "col", scatter_dimension=0, tiled=True)
        received = lax.all_to_all(
            reduced.reshape(n_row, share_rows, panel_width),
            "row",
            split_axis=0,
            concat_axis=0,
            tiled=True,
        )
        product = jnp.sum(received, axis=0)
        w_mine = lax.dynamic_slice_in_dim(w_loc, col_index * share_rows, share_rows, 0)
        own_term = jnp.dot(w_mine.T, product, precision=highest)
        summed_total = lax.psum(own_term, ("row", "col"))
        node_ends = jnp.cumsum(bounds[front_index])
        columns = jnp.arange(panel_width, dtype=jnp.int32)
        node_ids = jnp.sum((columns[:, None] >= node_ends[None, :]).astype(jnp.int32), axis=1)
        same_node = (node_ids[:, None] == node_ids[None, :]).astype(jnp.float32)
        borders.append(-product)
        diagonals.append(same_node * (diag_terms[front_index] + summed_total))
    return (jnp.stack(borders), jnp.stack(diagonals))


def solution(mesh):
    placed = (P("row", "col"), P(), P(None, "row", None), P(), P())
    return jax.shard_map(
        body,
        mesh=mesh,
        in_specs=placed,
        out_specs=(P(None, ("row", "col"), None), P()),
        check_vma=False,
    )
```

profile of v0, /device:TPU:0, one launch (start us, length us, event | category | flops | bytes accessed | tf_op | source)
XLA Modules:
  0.0 484.4 jit_solution(6554460476007873666)
XLA Ops:
  7.2 0.8 slice_reduce_fusion.1
  8.0 1.7 fusion.46
  10.0 2.3 fusion.6
  12.3 0.7 copy.51
  13.1 2.3 fusion.4
  15.5 0.7 copy.50
  17.2 15.4 %all-gather.3.cloned.1.call-done = f32[1024,256]{1,0:T(8,128)} async-done(((f32[256,256]{1,0:T(8,128)}), f32[1024,256]{1,0:T(8,128)}) %all-gather.3.cloned.1.call-update) | async-done | bytes 1048592 | tf_op jit(solution)/shard_map/all_gather | solution.py:31
  32.6 4.0 fusion.10
  37.4 58.5 %convolution_bitcast_fusion.1 = f32[4096,256]{0,1:T(8,128)} fusion(f32[2048,256]{1,0:T(8,128)S(1)} %bitcast.104, f32[4096,2048]{1,0:T(8,128)} %param.5), kind=kOutput, calls=%fused_computation.7 | convolution fusion | flops 25769803776 | bytes 39845888 | tf_op jit(solution)/shard_map/dot_general | solution.py:42
  95.9 6.6 %reshape.215 = f32[16,2,128,256]{2,1,0,3:T(2,128)} reshape(f32[4096,256]{0,1:T(8,128)} %convolution_bitcast_fusion.1) | data formatting | bytes 8388608 | tf_op jit(solution)/shard_map/reshape | solution.py:44
  102.5 9.3 %copy.20 = f32[16,2,128,256]{3,1,2,0:T(2,128)} copy(f32[16,2,128,256]{2,1,0,3:T(2,128)} %reshape.215) | data formatting | bytes 8388608 | tf_op jit(solution)/shard_map/reshape | solution.py:44
  111.8 11.7 %fusion.34 = f32[8,16,128,256]{3,0,2,1:T(8,128)S(1)} fusion(f32[16,2,128,256]{3,1,2,0:T(2,128)} %copy.20, s32[8]{0:T(128)S(1)} %and_select_fusion), kind=kOutput, calls=%fused_computation.58 | convolution fusion | flops 100663312 | bytes 20971552 | tf_op jit(solution)/shard_map/cq,kqap->ckap/dot_general | solution.py:52
  123.5 12.2 %fusion.2 = f32[8,4,128,256]{3,1,2,0:T(4,128)S(1)} fusion(f32[8,16,128,256]{3,0,2,1:T(8,128)S(1)} %fusion.34, s32[16]{0:T(128)S(1)} %iota_add_fusion.1, s32[8,4]{1,0:T(8,128)S(1)} %gather_fusion), kind=kOutput, calls=%fused_computation.4 | convolution fusion | flops 201327104 | bytes 20971712 | tf_op jit(solution)/shard_map/cdk,ckap->cdap/dot_general | solution.py:53
  135.7 2.7 copy.22
  139.1 4.0 fusion.8
  143.2 0.7 copy.25
  143.8 58.8 %convolution_bitcast_fusion = f32[4096,256]{0,1:T(8,128)} fusion(f32[2048,256]{1,0:T(8,128)S(1)} %bitcast.105, f32[4096,2048]{1,0:T(8,128)} %param.5), kind=kOutput, calls=%fused_computation.6 | convolution fusion | flops 25769803776 | bytes 39845888 | tf_op jit(solution)/shard_map/dot_general | solution.py:42
  202.6 6.7 %reshape.220 = f32[16,2,128,256]{2,1,0,3:T(2,128)} reshape(f32[4096,256]{0,1:T(8,128)} %convolution_bitcast_fusion) | data formatting | bytes 8388608 | tf_op jit(solution)/shard_map/reshape | solution.py:44
  209.3 9.3 %copy.26 = f32[16,2,128,256]{3,1,2,0:T(2,128)} copy(f32[16,2,128,256]{2,1,0,3:T(2,128)} %reshape.220) | data formatting | bytes 8388608 | tf_op jit(solution)/shard_map/reshape | solution.py:44
  218.6 11.7 %fusion.32 = f32[8,16,128,256]{3,0,2,1:T(8,128)S(1)} fusion(f32[16,2,128,256]{3,1,2,0:T(2,128)} %copy.26, s32[8]{0:T(128)S(1)} %and_select_fusion), kind=kOutput, calls=%fused_computation.56 | convolution fusion | flops 100663312 | bytes 20971552 | tf_op jit(solution)/shard_map/cq,kqap->ckap/dot_general | solution.py:52
  230.3 12.2 %fusion = f32[8,4,128,256]{3,1,2,0:T(4,128)S(1)} fusion(f32[8,16,128,256]{3,0,2,1:T(8,128)S(1)} %fusion.32, s32[8,4]{1,0:T(8,128)S(1)} %gather_fusion.1, s32[16]{0:T(128)S(1)} %iota_add_fusion.1), kind=kOutput, calls=%fused_computation.2 | convolution fusion | flops 201327104 | bytes 20971712 | tf_op jit(solution)/shard_map/cdk,ckap->cdap/dot_general | solution.py:53
  242.5 2.7 copy.28
  245.3 3.6 all-to-all-start
  249.4 84.5 %reduce-scatter.5.cloned.1.call-done = f32[512,256]{1,0:T(8,128)} async-done(((f32[4096,256]{1,0:T(8,128)}), f32[512,256]{1,0:T(8,128)}) %reduce-scatter.5.cloned.1.call-update) | async-done | bytes 524304 | tf_op jit(solution)/shard_map/reduce_scatter | solution.py:55
  333.9 3.5 all-to-all-start.1
  337.5 2.1 fusion.18
  339.5 6.6 %all-to-all-done.1 = f32[4,128,256]{2,1,0:T(8,128)S(1)} async-done(((f32[4,128,256]{2,1,0:T(8,128)}), f32[4,128,256]{2,1,0:T(8,128)S(1)}, u32[]{:S(2)}, u32[]{:S(2)}) %all-to-all-start.1) | async-done | bytes 524320 | tf_op jit(solution)/shard_map/all_to_all | solution.py:56
  346.2 1.1 fusion.16
  347.3 0.7 pad_maximum_fusion.1
  348.1 127.4 %all-reduce.3.cloned.1.call-done = (f32[256,256]{1,0:T(8,128)}, f32[256,256]{1,0:T(8,128)}) async-done(((f32[256,256]{1,0:T(8,128)}, f32[256,256]{1,0:T(8,128)}), (f32[256,256]{1,0:T(8,128)}, f32[256,256]{1,0:T(8,128)})) %all-reduce.3.cloned.1.call-update) | async-done | bytes 524304 | tf_op jit(solution)/shard_map/psum | solution.py:66
  475.5 1.2 fusion.15
  476.7 0.8 pad_maximum_fusion
  (42 shorter events, 3.4 us)
Async XLA Ops:
  7.2 25.5 %all-gather.3.cloned.1.call-start = ((), (), s32[]{:S(2)}) async-start(), calls=%async_computation.4 | async-start | bytes 1310720 | tf_op jit(solution)/shard_map/all_gather | solution.py:31
  9.7 27.7 %copy-start = (f32[1,1024,256]{2,1,0:T(8,128)}, f32[1,1024,256]{2,1,0:T(8,128)S(1)}, u32[]{:S(2)}) copy-start(f32[1,1024,256]{2,1,0:T(8,128)S(1)} %get-tuple-element.10) | copy-start | bytes 3145732
  13.1 126.1 %all-gather.5.cloned.1.call-start = ((), (), s32[]{:S(2)}) async-start(), calls=%async_computation.6 | async-start | bytes 1310720 | tf_op jit(solution)/shard_map/all_gather | solution.py:31
  16.2 229.1 %reduce-scatter.3.cloned.1.call-start = ((), (), s32[]{:S(2)}) async-start(), calls=%async_computation.5 | async-start | bytes 4718592 | tf_op jit(solution)/shard_map/reduce_scatter | solution.py:55
  138.4 195.5 %reduce-scatter.5.cloned.1.call-start = ((), (), s32[]{:S(2)}) async-start(), calls=%async_computation.7 | async-start | bytes 4718592 | tf_op jit(solution)/shard_map/reduce_scatter | solution.py:55
  245.2 3.7 copy-start.2
  245.2 230.3 %copy-start.1 = (f32[2,256,256]{2,1,0:T(8,128)S(1)}, f32[2,256,256]{2,1,0:T(8,128)}, u32[]{:S(2)}) copy-start(f32[2,256,256]{2,1,0:T(8,128)} %param.8) | copy-start | bytes 1572868
  245.3 88.6 %all-to-all-start = ((f32[4,128,256]{2,1,0:T(8,128)}), f32[4,128,256]{2,1,0:T(8,128)S(1)}, u32[]{:S(2)}, u32[]{:S(2)}) async-start(f32[4,128,256]{2,1,0:T(8,128)} %bitcast.112), calls=%async_computation.1 | async-start | bytes 1048576 | tf_op jit(solution)/shard_map/all_to_all | solution.py:56
  333.9 12.3 %all-to-all-start.1 = ((f32[4,128,256]{2,1,0:T(8,128)}), f32[4,128,256]{2,1,0:T(8,128)S(1)}, u32[]{:S(2)}, u32[]{:S(2)}) async-start(f32[4,128,256]{2,1,0:T(8,128)} %bitcast.113), calls=%async_computation.3 | async-start | bytes 1048576 | tf_op jit(solution)/shard_map/all_to_all | solution.py:56
  337.3 138.2 %all-reduce.3.cloned.1.call-start = ((), (), s32[]{:S(2)}) async-start(), calls=%async_computation.8 | async-start | bytes 1048576 | tf_op jit(solution)/shard_map/psum | solution.py:66
Sparse Core Ops, SparseCore 0:
  13.2 19.4 all-gather.2
  34.8 16.6 all-gather.4
  138.5 88.2 reduce-scatter.2
  245.4 88.4 reduce-scatter.4
  347.4 128.0 all-reduce.2
where the time goes:
time: 492 us; the launch traced here: 484 us
  waiting for transfers between devices  234 us (48%)
  matrix products  181 us (37%)
  local copies, waits for them, and re-layouts  44.1 us (9%)
  between operations  14.4 us (3%)
  starting transfers between devices  7.29 us (1%)
    psum x1, waiting for transfers between devices, body(): summed_total = lax.psum(own_term, ('row', 'col'))  127 us
    dot_general x2, matrix products, body(): full_rows = jnp.dot(inverse, w_tilde, precision=highest)  117 us
    reduce_scatter x2, waiting for transfers between devices, body(): reduced = lax.psum_scatter(ordered, 'col', scatter_dimension=0, tiled=True)  84.5 us
    reshape x4, local copies, waits for them, and re-layouts, body(): full_rows.reshape(row_group, quarters, share_rows, panel_width)  31.9 us
    dot_general x2, matrix products, body(): jnp.einsum('cdk,ckap->cdap', block_pick, sectioned, precision=highest)  24.4 us
    dot_general x2, matrix products, body(): jnp.einsum('cq,kqap->ckap', quarter_pick, full_pieces, precision=highest)  23.4 us
    all_gather x2, waiting for transfers between devices, body(): lax.all_gather(own_piece, 'row', axis=0, tiled=True)  15.4 us
  transfers between devices with their start and end apart: 7, of which 4 were waited for; matrix products, arithmetic and copies ran while one was open for 45% of the time, Pallas kernels for 0%

commit v1 on v0

--- a/solution.py
+++ b/solution.py
@@ -1,9 +1,17 @@
+import functools
 import jax
 import jax.numpy as jnp
 from jax import lax
 from jax.sharding import PartitionSpec as P
 
 BS = 256
+
+
+def unite_scales_over_axis(panel, device_axis, axis_name):
+    return lax.psum(lax.psum(panel, device_axis), axis_name=axis_name)
+
+
+try_all_streams_for = functools.partial(unite_scales_over_axis, device_axis="col", axis_name="row")
 
 
 def body(inverse, front_blocks, panels, diag_terms, bounds):
@@ -63,7 +71,7 @@
         product = jnp.sum(received, axis=0)
         w_mine = lax.dynamic_slice_in_dim(w_loc, col_index * share_rows, share_rows, 0)
         own_term = jnp.dot(w_mine.T, product, precision=highest)
-        summed_total = lax.psum(own_term, ("row", "col"))
+        summed_total = try_all_streams_for(own_term)
         node_ends = jnp.cumsum(bounds[front_index])
         columns = jnp.arange(panel_width, dtype=jnp.int32)
         node_ids = jnp.sum((columns[:, None] >= node_ends[None, :]).astype(jnp.int32), axis=1)

time: 492 us -> 471 us (0.957)
  waiting for transfers between devices: 234 us -> 212 us
    psum x1 -> x2, waiting for transfers between devices: 127 us -> 105 us  [unite_scales_over_axis(): return lax.psum(lax.psum(panel, device_axis), axis_name=axis_name)]
  transfers between devices with their start and end apart: 7 -> 8, of which waited for: 4 -> 5; matrix products, arithmetic and copies ran while one was open for 45% -> 47% of each run, Pallas kernels for 0% -> 0%
where the time goes in v1:
time: 471 us; the launch traced here: 463 us
  waiting for transfers between devices  212 us (45%)
  matrix products  181 us (38%)
  local copies, waits for them, and re-layouts  44.1 us (9%)
  between operations  14.7 us (3%)
  starting transfers between devices  7.33 us (2%)
    dot_general x2, matrix products, body(): full_rows = jnp.dot(inverse, w_tilde, precision=highest)  117 us
    psum x2, waiting for transfers between devices, unite_scales_over_axis(): return lax.psum(lax.psum(panel, device_axis), axis_name=axis_name)  105 us
    reduce_scatter x2, waiting for transfers between devices, body(): reduced = lax.psum_scatter(ordered, 'col', scatter_dimension=0, tiled=True)  85 us
    reshape x4, local copies, waits for them, and re-layouts, body(): full_rows.reshape(row_group, quarters, share_rows, panel_width)  31.9 us
    dot_general x2, matrix products, body(): jnp.einsum('cdk,ckap->cdap', block_pick, sectioned, precision=highest)  24.4 us
    dot_general x2, matrix products, body(): jnp.einsum('cq,kqap->ckap', quarter_pick, full_pieces, precision=highest)  23.4 us
    all_gather x2, waiting for transfers between devices, body(): lax.all_gather(own_piece, 'row', axis=0, tiled=True)  15.4 us
  transfers between devices with their start and end apart: 8, of which 5 were waited for; matrix products, arithmetic and copies ran while one was open for 47% of the time, Pallas kernels for 0%

profile of v1, /device:TPU:0, one launch (start us, length us, event | category | flops | bytes accessed | tf_op | source)
XLA Modules:
  0.0 463.2 jit_solution(5611014468856938280)
XLA Ops:
  7.2 0.8 slice_reduce_fusion.1
  8.0 1.7 fusion.46
  10.0 2.3 fusion.6
  12.3 0.7 copy.51
  13.1 2.3 fusion.4
  15.5 0.7 copy.50
  17.2 15.4 %all-gather.3.cloned.1.call-done = f32[1024,256]{1,0:T(8,128)} async-done(((f32[256,256]{1,0:T(8,128)}), f32[1024,256]{1,0:T(8,128)}) %all-gather.3.cloned.1.call-update) | async-done | bytes 1048592 | tf_op jit(solution)/shard_map/all_gather | solution.py:39
  32.6 4.0 fusion.10
  37.4 58.5 %convolution_bitcast_fusion.1 = f32[4096,256]{0,1:T(8,128)} fusion(f32[2048,256]{1,0:T(8,128)S(1)} %bitcast.104, f32[4096,2048]{1,0:T(8,128)} %param.5), kind=kOutput, calls=%fused_computation.7 | convolution fusion | flops 25769803776 | bytes 39845888 | tf_op jit(solution)/shard_map/dot_general | solution.py:50
  95.9 6.6 %reshape.215 = f32[16,2,128,256]{2,1,0,3:T(2,128)} reshape(f32[4096,256]{0,1:T(8,128)} %convolution_bitcast_fusion.1) | data formatting | bytes 8388608 | tf_op jit(solution)/shard_map/reshape | solution.py:52
  102.5 9.3 %copy.20 = f32[16,2,128,256]{3,1,2,0:T(2,128)} copy(f32[16,2,128,256]{2,1,0,3:T(2,128)} %reshape.215) | data formatting | bytes 8388608 | tf_op jit(solution)/shard_map/reshape | solution.py:52
  111.8 11.7 %fusion.34 = f32[8,16,128,256]{3,0,2,1:T(8,128)S(1)} fusion(f32[16,2,128,256]{3,1,2,0:T(2,128)} %copy.20, s32[8]{0:T(128)S(1)} %and_select_fusion), kind=kOutput, calls=%fused_computation.58 | convolution fusion | flops 100663312 | bytes 20971552 | tf_op jit(solution)/shard_map/cq,kqap->ckap/dot_general | solution.py:60
  123.5 12.2 %fusion.2 = f32[8,4,128,256]{3,1,2,0:T(4,128)S(1)} fusion(f32[8,16,128,256]{3,0,2,1:T(8,128)S(1)} %fusion.34, s32[16]{0:T(128)S(1)} %iota_add_fusion.1, s32[8,4]{1,0:T(8,128)S(1)} %gather_fusion), kind=kOutput, calls=%fused_computation.4 | convolution fusion | flops 201327104 | bytes 20971712 | tf_op jit(solution)/shard_map/cdk,ckap->cdap/dot_general | solution.py:61
  135.7 2.7 copy.22
  139.1 4.0 fusion.8
  143.8 58.8 %convolution_bitcast_fusion = f32[4096,256]{0,1:T(8,128)} fusion(f32[2048,256]{1,0:T(8,128)S(1)} %bitcast.105, f32[4096,2048]{1,0:T(8,128)} %param.5), kind=kOutput, calls=%fused_computation.6 | convolution fusion | flops 25769803776 | bytes 39845888 | tf_op jit(solution)/shard_map/dot_general | solution.py:50
  202.6 6.7 %reshape.220 = f32[16,2,128,256]{2,1,0,3:T(2,128)} reshape(f32[4096,256]{0,1:T(8,128)} %convolution_bitcast_fusion) | data formatting | bytes 8388608 | tf_op jit(solution)/shard_map/reshape | solution.py:52
  209.3 9.3 %copy.26 = f32[16,2,128,256]{3,1,2,0:T(2,128)} copy(f32[16,2,128,256]{2,1,0,3:T(2,128)} %reshape.220) | data formatting | bytes 8388608 | tf_op jit(solution)/shard_map/reshape | solution.py:52
  218.6 11.7 %fusion.32 = f32[8,16,128,256]{3,0,2,1:T(8,128)S(1)} fusion(f32[16,2,128,256]{3,1,2,0:T(2,128)} %copy.26, s32[8]{0:T(128)S(1)} %and_select_fusion), kind=kOutput, calls=%fused_computation.56 | convolution fusion | flops 100663312 | bytes 20971552 | tf_op jit(solution)/shard_map/cq,kqap->ckap/dot_general | solution.py:60
  230.3 12.2 %fusion = f32[8,4,128,256]{3,1,2,0:T(4,128)S(1)} fusion(f32[8,16,128,256]{3,0,2,1:T(8,128)S(1)} %fusion.32, s32[8,4]{1,0:T(8,128)S(1)} %gather_fusion.1, s32[16]{0:T(128)S(1)} %iota_add_fusion.1), kind=kOutput, calls=%fused_computation.2 | convolution fusion | flops 201327104 | bytes 20971712 | tf_op jit(solution)/shard_map/cdk,ckap->cdap/dot_general | solution.py:61
  242.5 2.7 copy.28
  245.3 3.6 all-to-all-start
  248.9 84.9 %reduce-scatter.5.cloned.1.call-done = f32[512,256]{1,0:T(8,128)} async-done(((f32[4096,256]{1,0:T(8,128)}), f32[512,256]{1,0:T(8,128)}) %reduce-scatter.5.cloned.1.call-update) | async-done | bytes 524304 | tf_op jit(solution)/shard_map/reduce_scatter | solution.py:63
  333.9 3.5 all-to-all-start.1
  337.4 2.0 fusion.18
  339.5 6.7 %all-to-all-done.1 = f32[4,128,256]{2,1,0:T(8,128)S(1)} async-done(((f32[4,128,256]{2,1,0:T(8,128)}), f32[4,128,256]{2,1,0:T(8,128)S(1)}, u32[]{:S(2)}, u32[]{:S(2)}) %all-to-all-start.1) | async-done | bytes 524320 | tf_op jit(solution)/shard_map/all_to_all | solution.py:64
  346.2 1.1 fusion.16
  347.8 71.1 %all-reduce.5.cloned.1.call-done = (f32[256,256]{1,0:T(8,128)}, f32[256,256]{1,0:T(8,128)}) async-done(((f32[256,256]{1,0:T(8,128)}, f32[256,256]{1,0:T(8,128)}), (f32[256,256]{1,0:T(8,128)}, f32[256,256]{1,0:T(8,128)})) %all-reduce.5.cloned.1.call-update) | async-done | bytes 524304 | tf_op jit(solution)/shard_map/psum | solution.py:11
  419.0 0.7 pad_maximum_fusion.1
  419.7 34.2 %all-reduce.7.cloned.1.call-done = (f32[256,256]{1,0:T(8,128)}, f32[256,256]{1,0:T(8,128)}) async-done(((f32[256,256]{1,0:T(8,128)}, f32[256,256]{1,0:T(8,128)}), (f32[256,256]{1,0:T(8,128)}, f32[256,256]{1,0:T(8,128)})) %all-reduce.7.cloned.1.call-update) | async-done | bytes 524304 | tf_op jit(solution)/shard_map/psum | solution.py:11
  453.9 1.2 fusion.15
  455.1 0.8 pad_maximum_fusion
  (45 shorter events, 4.2 us)
Async XLA Ops:
  7.2 25.5 %all-gather.3.cloned.1.call-start = ((), (), s32[]{:S(2)}) async-start(), calls=%async_computation.4 | async-start | bytes 1310720 | tf_op jit(solution)/shard_map/all_gather | solution.py:39
  9.7 27.7 %copy-start = (f32[1,1024,256]{2,1,0:T(8,128)}, f32[1,1024,256]{2,1,0:T(8,128)S(1)}, u32[]{:S(2)}) copy-start(f32[1,1024,256]{2,1,0:T(8,128)S(1)} %get-tuple-element.12) | copy-start | bytes 3145732
  13.1 126.1 %all-gather.5.cloned.1.call-start = ((), (), s32[]{:S(2)}) async-start(), calls=%async_computation.6 | async-start | bytes 1310720 | tf_op jit(solution)/shard_map/all_gather | solution.py:39
  16.2 229.1 %reduce-scatter.3.cloned.1.call-start = ((), (), s32[]{:S(2)}) async-start(), calls=%async_computation.5 | async-start | bytes 4718592 | tf_op jit(solution)/shard_map/reduce_scatter | solution.py:63
  138.4 195.5 %reduce-scatter.5.cloned.1.call-start = ((), (), s32[]{:S(2)}) async-start(), calls=%async_computation.7 | async-start | bytes 4718592 | tf_op jit(solution)/shard_map/reduce_scatter | solution.py:63
  245.2 102.1 %copy-start.2 = (s32[2,4]{1,0:T(2,128)S(1)}, s32[2,4]{1,0:T(2,128)}, u32[]{:S(2)}) copy-start(s32[2,4]{1,0:T(2,128)} %param.9) | copy-start | bytes 100
  245.3 208.7 %copy-start.1 = (f32[2,256,256]{2,1,0:T(8,128)S(1)}, f32[2,256,256]{2,1,0:T(8,128)}, u32[]{:S(2)}) copy-start(f32[2,256,256]{2,1,0:T(8,128)} %param.8) | copy-start | bytes 1572868
  245.3 88.6 %all-to-all-start = ((f32[4,128,256]{2,1,0:T(8,128)}), f32[4,128,256]{2,1,0:T(8,128)S(1)}, u32[]{:S(2)}, u32[]{:S(2)}) async-start(f32[4,128,256]{2,1,0:T(8,128)} %bitcast.112), calls=%async_computation.1 | async-start | bytes 1048576 | tf_op jit(solution)/shard_map/all_to_all | solution.py:64
  333.9 12.3 %all-to-all-start.1 = ((f32[4,128,256]{2,1,0:T(8,128)}), f32[4,128,256]{2,1,0:T(8,128)S(1)}, u32[]{:S(2)}, u32[]{:S(2)}) async-start(f32[4,128,256]{2,1,0:T(8,128)} %bitcast.113), calls=%async_computation.3 | async-start | bytes 1048576 | tf_op jit(solution)/shard_map/all_to_all | solution.py:64
  337.3 81.6 %all-reduce.5.cloned.1.call-start = ((), (), s32[]{:S(2)}) async-start(), calls=%async_computation.8 | async-start | bytes 1048576 | tf_op jit(solution)/shard_map/psum | solution.py:11
  347.3 106.6 %all-reduce.7.cloned.1.call-start = ((), (), s32[]{:S(2)}) async-start(), calls=%async_computation.9 | async-start | bytes 1048576 | tf_op jit(solution)/shard_map/psum | solution.py:11
Sparse Core Ops, SparseCore 0:
  13.2 19.4 all-gather.2
  34.8 16.6 all-gather.4
  138.5 88.2 reduce-scatter.2
  245.4 88.4 reduce-scatter.4
  347.4 71.4 all-reduce.4
  421.2 32.6 all-reduce.6
